TPU v7x, 256 devices: a whole 4x4x8 slice. The times are simulated.
256 devices in a mesh: tm: 4 (over x), rows: 64 (over y, z, core).
Axes of the slice: x: 4, y: 4, z: 8, core: 2. Of those that a mesh axis runs over, the one named last changes fastest.
Arguments:
- latent: bfloat16 [4, 64, 160, 512], P('tm', 'rows'), may hold values from -350 to 350, as said below
- norm_gain: float32 [512], replicated, may hold values from 0.1 to 1.9
- norm_bias: float32 [512], replicated, may hold values from -4 to 4
- conv_weight: bfloat16 [3, 3, 3, 512, 512], P(None, None, None, 'rows', 'tm'), may hold values from -0.0546875 to 0.0546875
- cotangent: bfloat16 [4, 128, 320, 512], P('tm', 'rows'), may hold values from -180 to 180
Outputs:
- latent_grad: float32 [4, 64, 160, 512], P('tm', 'rows')
- gain_grad: float32 [512], replicated
- bias_grad: float32 [512], replicated
Inputs may be any that keep to these rules, and one draw needn't show every extreme that they name: `latent`: features of the unit's input.
All inputs are finite; a program needn't handle non-finite values.
Results may differ from a plain program's by a relative error of at most 0.0003.
Values may be sent and summed in bfloat16 or wider, within the bound.
No kernel may reach another device: no remote copies, remote signals or barrier semaphores. Data moves between devices by JAX's collectives and lax.ppermute only.
A program may use at most 320 MiB of HBM per device.

v0:
```python
import jax
import jax.numpy as jnp
from jax import lax
from jax.sharding import PartitionSpec as P

GROUPS = 32


def extended(block, sides, width):
    for axis, dim in sides:
        count = lax.axis_size(axis)
        forward = [(i, i + 1) for i in range(count - 1)]
        backward = [(target, source) for source, target in forward]
        low = lax.ppermute(
            lax.slice_in_dim(block, block.shape[dim] - width, None, axis=dim), axis, forward
        )
        high = lax.ppermute(lax.slice_in_dim(block, 0, width, axis=dim), axis, backward)
        block = jnp.concatenate([low, block, high], axis=dim)
    return block


def from_behind(value, axis, steps):
    count = lax.axis_size(axis)
    first, last = (max(0, -steps), min(count, count - steps))
    return lax.ppermute(value, axis, [(source, source + steps) for source in range(first, last)])


def shifted_rows(frames, extra_frames):
    padded = jnp.pad(frames, ((0, extra_frames), (0, 0), (1, 1), (0, 0)))
    fine_rows = frames.shape[1] - 2
    return [padded[:, 2 - row_tap : 2 - row_tap + fine_rows] for row_tap in range(3)]


def tap_total(row_slabs, weights, tap_pairs, frames_out, span_cols):
    running = None
    for offset, tap_index in tap_pairs:
        for row_tap in range(3):
            source = row_slabs[row_tap][offset : offset + frames_out]
            for col_tap in range(3):
                product = lax.dot_general(
                    source,
                    weights[tap_index, row_tap, col_tap],
                    (((3,), (1,)), ((), ())),
                    preferred_element_type=jnp.float32,
                )
                piece = product[:, :, 2 - col_tap : 2 - col_tap + span_cols, :]
                running = piece if running is None else running + piece
    return running


def pool_pairs(fine_grad):
    frames, fine_rows, span_cols, channels = fine_grad.shape
    return fine_grad.reshape(frames, fine_rows // 2, 2, span_cols // 2, 2, channels).sum(
        axis=(2, 4)
    )


def block_grad(row_slabs, weights, frames_out, first_frame):
    span_cols = row_slabs[0].shape[2] - 2

    def extra_terms():
        return tap_total(row_slabs, weights, ((0, 1), (0, 0), (1, 0)), 1, span_cols)

    def no_terms():
        return jnp.zeros((1, row_slabs[0].shape[1], span_cols, weights.shape[3]), jnp.float32)

    main_part = tap_total(row_slabs, weights, ((0, 2), (1, 1), (2, 0)), frames_out, span_cols)
    main_part = main_part + lax.cond(first_frame, extra_terms, no_terms)
    return pool_pairs(main_part)


def on_device(latent, norm_gain, norm_bias, conv_weight, cotangent):
    frames_all = lax.axis_size("tm")
    rows_all = lax.axis_size("rows")
    low_rows = latent.shape[1]
    low_cols = latent.shape[2]
    channels = latent.shape[3]
    per_group = channels // GROUPS
    cell_count = frames_all * rows_all * low_rows * low_cols
    rimmed = extended(cotangent, (("rows", 1),), 1)
    following = from_behind(rimmed, "tm", -1)
    further = from_behind(rimmed, "tm", -2)
    stacked = jnp.concatenate([rimmed, following, further], axis=0)
    weight_wide = lax.all_gather(conv_weight, "tm", axis=4, tiled=True)
    weight_full = lax.all_gather(weight_wide, "rows", axis=3, tiled=True)
    up_grad = block_grad(shifted_rows(stacked, 0), weight_full, 1, lax.axis_index("tm") == 0)
    features = latent.astype(jnp.float32)
    sum_x = jnp.sum(features, axis=(0, 1, 2))
    sum_sq = jnp.sum(features * features, axis=(0, 1, 2))
    total_x, total_sq = lax.psum((sum_x, sum_sq), ("tm", "rows"))
    group_x = total_x.reshape(GROUPS, per_group).sum(axis=1)
    group_sq = total_sq.reshape(GROUPS, per_group).sum(axis=1)
    group_mean = group_x / (cell_count * per_group)
    group_var = group_sq / (cell_count * per_group) - group_mean * group_mean
    inv_std = lax.rsqrt(group_var + 1e-06)
    mean_chan = jnp.repeat(group_mean, per_group)
    inv_chan = jnp.repeat(inv_std, per_group)
    normed = (features - mean_chan) * inv_chan
    pre = normed * norm_gain + norm_bias
    sigmoid_pre = jax.nn.sigmoid(pre)
    act_grad = up_grad * sigmoid_pre * (1.0 + pre * (1.0 - sigmoid_pre))
    sum_act, sum_scaled = lax.psum(
        (jnp.sum(act_grad, axis=(0, 1, 2)), jnp.sum(act_grad * normed, axis=(0, 1, 2))),
        ("tm", "rows"),
    )
    gain_grad = sum_scaled / cell_count
    bias_grad = sum_act / cell_count
    mean_q = (norm_gain * sum_act).reshape(GROUPS, per_group).sum(axis=1) / (cell_count * per_group)
    mean_qn = (norm_gain * sum_scaled).reshape(GROUPS, per_group).sum(axis=1) / (
        cell_count * per_group
    )
    latent_grad = inv_chan * (
        act_grad * norm_gain
        - jnp.repeat(mean_q, per_group)
        - normed * jnp.repeat(mean_qn, per_group)
    )
    return (latent_grad, gain_grad, bias_grad)


def solution(mesh):
    placed = (
        P("tm", "rows", None, None),
        P(),
        P(),
        P(None, None, None, "rows", "tm"),
        P("tm", "rows", None, None),
    )
    return jax.shard_map(
        on_device,
        mesh=mesh,
        in_specs=placed,
        out_specs=(P("tm", "rows", None, None), P(), P()),
        check_vma=False,
    )
```

profile of v0, /device:TPU:1, one launch (start us, length us, event | category | flops | bytes accessed | tf_op | source)
XLA Modules:
  0.0 354.6 jit_solution(4041163253013684087)
XLA Ops:
  7.2 11.7 %all_gather.6 = bf16[3,3,3,8,512]{4,3,2,1,0:T(8,128)(2,1)} all-gather(bf16[3,3,3,8,128]{4,3,2,1,0:T(8,128)(2,1)} %param.10), channel_id=1, replica_groups=mesh['tm'=4,'rows'=64] {'tm'}, dimensions={4}, use_global_device_ids=true | all-gather | bytes 276480 | tf_op jit(solution)/shard_map/all_gather | solution.py:84
  18.9 1.1 fusion.134
  20.1 6.2 %collective-permute-start = (bf16[1,1,320,512]{3,2,1,0:T(8,128)(2,1)S(1)}, bf16[1,1,320,512]{3,2,1,0:T(8,128)(2,1)S(1)}, u32[]{:S(2)}, u32[]{:S(2)}) collective-permute-start(bf16[1,1,320,512]{3,2,1,0:T(8,128)(2,1)S(1)} %get-tuple-element.27), channel_id=1, source_target_pairs={{0,1},{1,2},{2,3},{3,4},{4,5},{5,6},{6,7},{7,8},{8,9},{9,10},{10,1... | collective-permute-start | bytes 983048 | tf_op jit(solution)/shard_map/ppermute | solution.py:14
  26.3 1.9 collective-permute-start.1
  28.2 2.1 collective-permute-done
  30.4 4.3 %collective-permute-done.1 = bf16[1,1,320,512]{3,2,1,0:T(8,128)(2,1)S(1)} collective-permute-done((bf16[1,1,320,512]{3,2,1,0:T(8,128)(2,1)S(1)}, bf16[1,1,320,512]{3,2,1,0:T(8,128)(2,1)S(1)}, u32[]{:S(2)}, u32[]{:S(2)}) %collective-permute-start.1) | collective-permute-done | bytes 327712 | tf_op jit(solution)/shard_map/ppermute | solution.py:17
  34.7 1.3 collective-permute-start.3
  36.0 1.3 collective-permute-start.2
  37.6 129.7 %all-reduce.2 = (f32[32,16]{1,0:T(8,128)S(1)}, f32[32,16]{1,0:T(8,128)S(1)}) all-reduce(f32[32,16]{1,0:T(8,128)S(1)} %reshape.178, f32[32,16]{1,0:T(8,128)S(1)} %reshape.177), channel_id=1, replica_groups=mesh['tm'=4,'rows'=64] {'tm','rows'}, use_global_device_ids=true, to_apply=%region_4.5 | all-reduce | flops 1024 | bytes 8192 | tf_op jit(solution)/shard_map/psum | solution.py:90
  167.8 3.9 %fusion.113 = bf16[3,4,322,512]{3,2,1,0:T(8,128)(2,1)} fusion(bf16[1,4,320,512]{3,2,1,0:T(8,128)(2,1)} %collective-permute-done.3, bf16[1,4,320,512]{3,2,1,0:T(8,128)(2,1)} %collective-permute-done.2, bf16[1,4,320,512]{3,2,1,0:T(8,128)(2,1)S(1)} %constant_dynamic-update-slice_fusion), kind=kLoop, calls=%fused_computation.168 | loop fusion | flops 23740416 | bytes 7888896 | tf_op jit(solution)/shard_map/concatenate | solution.py:83
  171.7 48.1 %conditional.1 = (f32[1,2,320,512]{3,2,1,0:T(8,128)}) conditional(s32[]{:T(128)} %convert_element_type.9, () %tuple.14, (bf16[3,4,322,512]{3,2,1,0:T(8,128)(2,1)}, bf16[3,3,3,512,512]{4,3,2,1,0:T(8,128)(2,1)}) %tuple.15), branch_computations={%region_6.7_spmd, %region_7.8_spmd} | conditional | flops 9124839424 | bytes 177053760 | solution.py:68
  171.7 1.9 convolution_bitcast_fusion.15
  173.6 1.8 convolution_bitcast_fusion.16
  175.5 1.7 convolution_bitcast_fusion.17
  177.2 2.0 convolution_bitcast_fusion.24
  179.2 2.1 convolution_bitcast_fusion.25
  181.4 1.6 convolution_bitcast_fusion.12
  183.0 1.6 convolution_bitcast_fusion.13
  184.6 1.6 convolution_bitcast_fusion.14
  186.7 0.5 convolution_bitcast_fusion.22
  187.8 0.5 convolution_bitcast_fusion.10
  188.3 0.5 convolution_bitcast_fusion.11
  189.4 1.6 convolution_bitcast_fusion.19
  191.0 1.6 convolution_bitcast_fusion.6
  192.7 1.6 convolution_bitcast_fusion.7
  194.3 1.7 convolution_bitcast_fusion.3
  195.9 1.6 convolution_bitcast_fusion.4
  197.5 1.6 convolution_bitcast_fusion
  199.2 1.6 convolution_bitcast_fusion.1
  200.8 1.6 convolution_bitcast_fusion.2
  202.4 1.7 convolution_bitcast_fusion.5
  204.1 1.7 convolution_bitcast_fusion.8
  205.8 1.7 convolution_bitcast_fusion.20
  207.5 1.6 convolution_bitcast_fusion.23
  209.1 1.6 convolution_bitcast_fusion.26
  210.7 9.0 %slice_add_fusion = f32[1,2,320,512]{3,2,1,0:T(8,128)} fusion(f32[1,2,322,512]{3,2,1,0:T(8,128)} %convolution_bitcast_fusion, f32[1,2,322,512]{3,2,1,0:T(8,128)} %convolution_bitcast_fusion.1, f32[1,2,322,512]{3,2,1,0:T(8,128)} %convolution_bitcast_fusion.2, f32[1,2,322,512]{3,2,1,0:T(8,128)} %convolution_bitcast_fusion.3, ...), kind=kLoop, calls=%fused_computation.27 | loop fusion | flops 8519680 | bytes 36700160 | tf_op jit(solution)/shard_map/cond/branch_1_fun/add | solution.py:47
  219.8 1.9 convolution_bitcast_fusion.28
  221.7 1.8 convolution_bitcast_fusion.27
  223.6 1.7 convolution_bitcast_fusion.31
  225.3 2.0 convolution_bitcast_fusion.30
  227.3 2.1 convolution_bitcast_fusion.34
  229.5 1.6 convolution_bitcast_fusion.33
  231.1 1.6 convolution_bitcast_fusion.37
  232.7 1.6 convolution_bitcast_fusion.36
  237.0 1.7 convolution_bitcast_fusion.45
  238.7 1.7 convolution_bitcast_fusion.49
  240.4 1.6 convolution_bitcast_fusion.48
  242.0 1.6 convolution_bitcast_fusion.52
  243.6 1.6 convolution_bitcast_fusion.51
  245.2 1.6 convolution_bitcast_fusion.29
  246.9 1.6 convolution_bitcast_fusion.32
  248.5 1.6 convolution_bitcast_fusion.35
  250.1 1.6 convolution_bitcast_fusion.38
  251.7 1.7 convolution_bitcast_fusion.41
  253.4 1.6 convolution_bitcast_fusion.44
  255.0 1.6 convolution_bitcast_fusion.47
  256.6 1.6 convolution_bitcast_fusion.50
  258.2 1.7 convolution_bitcast_fusion.53
  259.9 10.1 %fusion.115 = f32[320,512]{1,0:T(8,128)} fusion(f32[1,2,320,512]{3,2,1,0:T(8,128)} %get-tuple-element.34, f32[1,2,322,512]{3,2,1,0:T(8,128)S(1)} %convolution_bitcast_fusion.27, f32[1,2,322,512]{3,2,1,0:T(8,128)S(1)} %convolution_bitcast_fusion.28, f32[1,2,322,512]{3,2,1,0:T(8,128)} %convolution_bitcast_fusion.29, ...), kind=kLoop, calls=%fused_computation.198 | loop fusion | flops 9011200 | bytes 37355520 | tf_op jit(solution)/shard_map/reduce_sum | solution.py:53
  270.0 1.5 reduce_sum.95
  271.5 0.8 reduce_sum.96
  272.5 73.1 %all-reduce.1 = (f32[512]{0:T(512)S(1)}, f32[512]{0:T(512)S(1)}) all-reduce(f32[512]{0:T(512)S(1)} %get-tuple-element.18, f32[512]{0:T(512)S(1)} %get-tuple-element.17), channel_id=1, replica_groups=mesh['tm'=4,'rows'=64] {'tm','rows'}, use_global_device_ids=true, to_apply=%region_14.15 | all-reduce | flops 1024 | bytes 8192 | tf_op jit(solution)/shard_map/psum | solution.py:102
  345.6 0.6 broadcast_multiply_fusion
  346.9 0.8 fusion.131
  (53 shorter events, 6.2 us)
Async XLA Ops:
  7.2 23.2 %copy-start.4 = (bf16[1,2,320,512]{3,2,1,0:T(8,128)(2,1)S(1)}, bf16[1,2,320,512]{3,2,1,0:T(8,128)(2,1)}, u32[]{:S(2)}) copy-start(bf16[1,2,320,512]{3,2,1,0:T(8,128)(2,1)} %param.11) | copy-start | bytes 1966084
  7.2 164.5 %all-gather.2.cloned.1.call-start = ((), (), s32[]{:S(2)}) async-start(), calls=%async_computation | async-start | bytes 14376960 | tf_op jit(solution)/shard_map/all_gather | solution.py:85
  20.0 17.3 %copy-start.5 = (bf16[1,1,160,512]{3,2,1,0:T(8,128)(2,1)S(1)}, bf16[1,1,160,512]{3,2,1,0:T(8,128)(2,1)}, u32[]{:S(2)}) copy-start(bf16[1,1,160,512]{3,2,1,0:T(8,128)(2,1)} %param.7) | copy-start | bytes 491524
  20.1 10.2 %collective-permute-start = (bf16[1,1,320,512]{3,2,1,0:T(8,128)(2,1)S(1)}, bf16[1,1,320,512]{3,2,1,0:T(8,128)(2,1)S(1)}, u32[]{:S(2)}, u32[]{:S(2)}) collective-permute-start(bf16[1,1,320,512]{3,2,1,0:T(8,128)(2,1)S(1)} %get-tuple-element.27), channel_id=1, source_target_pairs={{0,1},{1,2},{2,3},{3,4},{4,5},{5,6},{6,7},{7,8},{8,9},{9,10},{10,1... | collective-permute-start | bytes 983048 | tf_op jit(solution)/shard_map/ppermute | solution.py:14
  26.3 8.4 %collective-permute-start.1 = (bf16[1,1,320,512]{3,2,1,0:T(8,128)(2,1)S(1)}, bf16[1,1,320,512]{3,2,1,0:T(8,128)(2,1)S(1)}, u32[]{:S(2)}, u32[]{:S(2)}) collective-permute-start(bf16[1,1,320,512]{3,2,1,0:T(8,128)(2,1)S(1)} %get-tuple-element.26), channel_id=1, source_target_pairs={{1,0},{2,1},{3,2},{4,3},{5,4},{6,5},{7,6},{8,7},{9,8},{10,9},{11,1... | collective-permute-start | bytes 983048 | tf_op jit(solution)/shard_map/ppermute | solution.py:17
  34.7 133.1 %collective-permute-start.3 = (bf16[1,4,320,512]{3,2,1,0:T(8,128)(2,1)S(1)}, bf16[1,4,320,512]{3,2,1,0:T(8,128)(2,1)}, u32[]{:S(2)}, u32[]{:S(2)}) collective-permute-start(bf16[1,4,320,512]{3,2,1,0:T(8,128)(2,1)S(1)} %constant_dynamic-update-slice_fusion), channel_id=1, source_target_pairs={{128,0},{192,64},{129,1},{193,65},{130,2},{194,66},{131,3},{195,67... | collective-permute-start | bytes 3932168 | tf_op jit(solution)/shard_map/ppermute | solution.py:25
  36.0 131.8 %collective-permute-start.2 = (bf16[1,4,320,512]{3,2,1,0:T(8,128)(2,1)S(1)}, bf16[1,4,320,512]{3,2,1,0:T(8,128)(2,1)}, u32[]{:S(2)}, u32[]{:S(2)}) collective-permute-start(bf16[1,4,320,512]{3,2,1,0:T(8,128)(2,1)S(1)} %constant_dynamic-update-slice_fusion), channel_id=1, source_target_pairs={{64,0},{128,64},{192,128},{65,1},{129,65},{193,129},{66,2},{130,66... | collective-permute-start | bytes 3932168 | tf_op jit(solution)/shard_map/ppermute | solution.py:25
  171.7 3.7 %copy-start.1 = (bf16[3,4,322,512]{3,2,1,0:T(8,128)(2,1)S(1)}, bf16[3,4,322,512]{3,2,1,0:T(8,128)(2,1)}, u32[]{:S(2)}) copy-start(bf16[3,4,322,512]{3,2,1,0:T(8,128)(2,1)} %get-tuple-element.12) | copy-start | bytes 11870212 | tf_op jit(solution)/shard_map/cond
  175.4 10.7 %copy-start.3 = (bf16[3,3,3,512,512]{4,3,2,1,0:T(8,128)(2,1)S(1)}, bf16[3,3,3,512,512]{4,3,2,1,0:T(8,128)(2,1)}, u32[]{:S(2)}) copy-start(bf16[3,3,3,512,512]{4,3,2,1,0:T(8,128)(2,1)} %get-tuple-element.13) | copy-start | bytes 42467332 | tf_op jit(solution)/shard_map/cond
  219.8 3.7 %copy-start = (bf16[3,4,322,512]{3,2,1,0:T(8,128)(2,1)S(1)}, bf16[3,4,322,512]{3,2,1,0:T(8,128)(2,1)}, u32[]{:S(2)}) copy-start(bf16[3,4,322,512]{3,2,1,0:T(8,128)(2,1)} %fusion.113) | copy-start | bytes 11870212
  223.5 10.7 %copy-start.2 = (bf16[3,3,3,512,512]{4,3,2,1,0:T(8,128)(2,1)S(1)}, bf16[3,3,3,512,512]{4,3,2,1,0:T(8,128)(2,1)}, u32[]{:S(2)}) copy-start(bf16[3,3,3,512,512]{4,3,2,1,0:T(8,128)(2,1)} %all-gather.2.cloned.1.call-done) | copy-start | bytes 42467332
  270.0 2.3 copy-start.6
  270.0 2.3 copy-start.7
Sparse Core Ops, SparseCore 0:
  19.0 105.3 all-gather.1
where the time goes:
time: 355 us
  blocking collectives  214 us (60%)
  matrix products  78.8 us (22%)
  other arithmetic  26 us (7%)
  between operations  14.3 us (4%)
  starting transfers between devices  10.8 us (3%)
  waiting for transfers between devices  6.41 us (2%)
  local copies, waits for them, and re-layouts  3.66 us (1%)
    psum x1, blocking collectives, on_device(): total_x, total_sq = lax.psum((sum_x, sum_sq), ('tm', 'rows'))  130 us
    dot_general x54, matrix products, tap_total(): lax.dot_general(source, weights[tap_index, row_tap, col_tap], (((3,), (1,...  78.8 us
    psum x1, blocking collectives, on_device(): lax.psum((jnp.sum(act_grad, axis=(0, 1, 2)), jnp.sum(act_grad * normed, a...  73.1 us
    all_gather x1, blocking collectives, on_device(): weight_wide = lax.all_gather(conv_weight, 'tm', axis=4, tiled=True)  11.7 us
    reduce_sum x2, other arithmetic, pool_pairs(): fine_grad.reshape(frames, fine_rows // 2, 2, span_cols // 2, 2, channels)  10.9 us
    add x1, other arithmetic, tap_total(): running = piece if running is None else running + piece  9.05 us
  transfers between devices with their start and end apart: 5, of which 2 were waited for; matrix products, arithmetic and copies ran while one was open for 2% of the time, Pallas kernels for 0%

commit v1 on v0

--- a/solution.py
+++ b/solution.py
@@ -4,6 +4,13 @@
 from jax.sharding import PartitionSpec as P
 
 GROUPS = 32
+
+
+def gather_over(value, axis, dim):
+    n_dev = lax.axis_size(axis)
+    tiles = jnp.stack([value for _ in range(n_dev)])
+    tiles = lax.all_to_all(tiles, axis, split_axis=0, concat_axis=0)
+    return jnp.concatenate(tiles, axis=dim)
 
 
 def extended(block, sides, width):
@@ -82,7 +89,7 @@
     further = from_behind(rimmed, "tm", -2)
     stacked = jnp.concatenate([rimmed, following, further], axis=0)
     weight_wide = lax.all_gather(conv_weight, "tm", axis=4, tiled=True)
-    weight_full = lax.all_gather(weight_wide, "rows", axis=3, tiled=True)
+    weight_full = gather_over(weight_wide, "rows", 3)
     up_grad = block_grad(shifted_rows(stacked, 0), weight_full, 1, lax.axis_index("tm") == 0)
     features = latent.astype(jnp.float32)
     sum_x = jnp.sum(features, axis=(0, 1, 2))

time: 355 us -> 658 us (1.85)
  waiting for transfers between devices: 6.41 us -> 304 us
  between operations: 14.3 us -> 0.88 us
  starting transfers between devices: 10.8 us -> 22.5 us
  local copies, waits for them, and re-layouts: 3.66 us -> 14.5 us
    ppermute x1, waiting for transfers between devices: 2.07 us -> 302 us  [extended(): lax.ppermute(lax.slice_in_dim(block, block.shape[dim] - width, None, axis...]
    all_to_all x0 -> x1, starting transfers between devices: none -> 14.3 us  [gather_over(): tiles = lax.all_to_all(tiles, axis, split_axis=0, concat_axis=0)]
    reshape x0 -> x1, local copies, waits for them, and re-layouts: none -> 7.04 us  [gather_over(): return jnp.concatenate(tiles, axis=dim)]
  transfers between devices with their start and end apart: 5 -> 5, of which waited for: 2 -> 2; matrix products, arithmetic and copies ran while one was open for 2% -> 1% of each run, Pallas kernels for 0% -> 0%
where the time goes in v1:
time: 658 us
  waiting for transfers between devices  304 us (46%)
  blocking collectives  212 us (32%)
  matrix products  74.1 us (11%)
  other arithmetic  30.3 us (5%)
  starting transfers between devices  22.5 us (3%)
  local copies, waits for them, and re-layouts  14.5 us (2%)
    ppermute x1, waiting for transfers between devices, extended(): lax.ppermute(lax.slice_in_dim(block, block.shape[dim] - width, None, axis...  302 us
    psum x1, blocking collectives, on_device(): total_x, total_sq = lax.psum((sum_x, sum_sq), ('tm', 'rows'))  127 us
    dot_general x54, matrix products, tap_total(): lax.dot_general(source, weights[tap_index, row_tap, col_tap], (((3,), (1,...  74.1 us
    psum x1, blocking collectives, on_device(): lax.psum((jnp.sum(act_grad, axis=(0, 1, 2)), jnp.sum(act_grad * normed, a...  73.4 us
    all_to_all x1, starting transfers between devices, gather_over(): tiles = lax.all_to_all(tiles, axis, split_axis=0, concat_axis=0)  14.3 us
    reduce_sum x2, other arithmetic, pool_pairs(): fine_grad.reshape(frames, fine_rows // 2, 2, span_cols // 2, 2, channels)  14.1 us
  transfers between devices with their start and end apart: 5, of which 2 were waited for; matrix products, arithmetic and copies ran while one was open for 1% of the time, Pallas kernels for 0%

profile of v1, /device:TPU:1, one launch (start us, length us, event | category | flops | bytes accessed | tf_op | source)
XLA Modules:
  0.0 657.9 jit_solution(5840074737089318877)
XLA Ops:
  0.6 11.1 %all_gather.3 = bf16[3,3,3,8,512]{4,3,2,1,0:T(8,128)(2,1)S(1)} all-gather(bf16[3,3,3,8,128]{4,3,2,1,0:T(8,128)(2,1)} %param.10), channel_id=1, replica_groups=mesh['tm'=4,'rows'=64] {'tm'}, dimensions={4}, use_global_device_ids=true | all-gather | bytes 276480 | tf_op jit(solution)/shard_map/all_gather | solution.py:91
  11.8 6.0 stack.2
  17.8 14.3 %all-to-all-start = ((bf16[64,3,3,3,8,512]{5,4,3,2,1,0:T(8,128)(2,1)}), bf16[64,3,3,3,8,512]{5,4,3,2,1,0:T(8,128)(2,1)}, u32[]{:S(2)}, u32[]{:S(2)}) async-start(bf16[64,3,3,3,8,512]{5,4,3,2,1,0:T(8,128)(2,1)} %stack.2), calls=%async_computation | async-start | bytes 28311552 | tf_op jit(solution)/shard_map/all_to_all | solution.py:12
  32.2 3.7 collective-permute-start
  35.9 1.9 collective-permute-start.1
  37.8 301.6 %collective-permute-done = bf16[1,1,320,512]{3,2,1,0:T(8,128)(2,1)S(1)} collective-permute-done((bf16[1,1,320,512]{3,2,1,0:T(8,128)(2,1)S(1)}, bf16[1,1,320,512]{3,2,1,0:T(8,128)(2,1)S(1)}, u32[]{:S(2)}, u32[]{:S(2)}) %collective-permute-start) | collective-permute-done | bytes 327712 | tf_op jit(solution)/shard_map/ppermute | solution.py:21
  339.5 2.1 collective-permute-done.1
  341.6 1.3 collective-permute-start.3
  342.9 1.3 collective-permute-start.2
  344.4 127.1 %all-reduce.2 = (f32[32,16]{1,0:T(8,128)S(1)}, f32[32,16]{1,0:T(8,128)S(1)}) all-reduce(f32[32,16]{1,0:T(8,128)S(1)} %reshape.186, f32[32,16]{1,0:T(8,128)S(1)} %reshape.185), channel_id=1, replica_groups=mesh['tm'=4,'rows'=64] {'tm','rows'}, use_global_device_ids=true, to_apply=%region_4.5 | all-reduce | flops 1024 | bytes 8192 | tf_op jit(solution)/shard_map/psum | solution.py:97
  472.1 3.7 fusion.113
  475.8 7.0 %copy_bitcast_fusion = bf16[3,3,3,512,512]{4,3,2,1,0:T(8,128)(2,1)S(1)} fusion(bf16[64,3,3,3,8,512]{5,4,3,2,1,0:T(8,128)(2,1)} %all-to-all-done), kind=kLoop, calls=%fused_computation.161 | loop fusion | bytes 28311552 | tf_op jit(solution)/shard_map/reshape | solution.py:13
  484.0 1.6 convolution_bitcast_fusion.29
  485.6 1.6 convolution_bitcast_fusion.30
  487.2 1.6 convolution_bitcast_fusion.31
  488.8 1.6 convolution_bitcast_fusion.32
  490.5 1.7 convolution_bitcast_fusion.33
  492.1 1.6 convolution_bitcast_fusion.34
  493.7 1.7 convolution_bitcast_fusion.35
  495.4 1.6 convolution_bitcast_fusion.36
  497.0 1.6 convolution_bitcast_fusion.37
  498.7 1.7 convolution_bitcast_fusion.38
  500.3 1.6 convolution_bitcast_fusion.39
  502.0 1.6 convolution_bitcast_fusion.40
  503.6 1.6 convolution_bitcast_fusion.41
  505.2 1.6 convolution_bitcast_fusion.42
  506.9 1.6 convolution_bitcast_fusion.43
  508.5 1.6 convolution_bitcast_fusion.44
  510.1 1.7 convolution_bitcast_fusion.45
  511.8 1.7 convolution_bitcast_fusion.46
  513.4 1.7 convolution_bitcast_fusion.47
  515.1 1.7 convolution_bitcast_fusion.48
  516.8 1.6 convolution_bitcast_fusion.49
  518.4 1.6 convolution_bitcast_fusion.50
  520.1 1.7 convolution_bitcast_fusion.51
  521.7 1.6 convolution_bitcast_fusion.52
  523.3 1.7 convolution_bitcast_fusion.53
  525.0 42.6 %conditional.1 = (f32[1,2,320,512]{3,2,1,0:T(8,128)}) conditional(s32[]{:T(128)} %convert_element_type.9, () %tuple.14, (bf16[3,4,322,512]{3,2,1,0:T(8,128)(2,1)S(1)}, bf16[3,3,3,512,512]{4,3,2,1,0:T(8,128)(2,1)S(1)}) %tuple.27), branch_computations={%region_6.7_spmd, %region_7.8_spmd} | conditional | flops 9124839424 | bytes 104603656 | solution.py:75
  525.5 0.5 convolution_bitcast_fusion.16
  526.1 0.5 convolution_bitcast_fusion.17
  527.7 0.5 convolution_bitcast_fusion.12
  530.5 0.5 convolution_bitcast_fusion.9
  531.0 1.6 convolution_bitcast_fusion.10
  532.7 1.7 convolution_bitcast_fusion.11
  534.3 1.6 convolution_bitcast_fusion.18
  535.9 1.7 convolution_bitcast_fusion.19
  537.6 1.6 convolution_bitcast_fusion.6
  539.2 1.7 convolution_bitcast_fusion.7
  540.9 1.6 convolution_bitcast_fusion.3
  542.6 1.6 convolution_bitcast_fusion.4
  544.2 1.6 convolution_bitcast_fusion
  545.8 1.6 convolution_bitcast_fusion.1
  547.4 1.6 convolution_bitcast_fusion.2
  549.0 1.6 convolution_bitcast_fusion.5
  550.7 1.6 convolution_bitcast_fusion.8
  552.2 1.6 convolution_bitcast_fusion.20
  553.9 1.6 convolution_bitcast_fusion.23
  555.5 1.7 convolution_bitcast_fusion.26
  557.1 10.2 %slice_add_fusion = f32[1,2,320,512]{3,2,1,0:T(8,128)} fusion(f32[1,2,322,512]{3,2,1,0:T(8,128)} %convolution_bitcast_fusion, f32[1,2,322,512]{3,2,1,0:T(8,128)} %convolution_bitcast_fusion.1, f32[1,2,322,512]{3,2,1,0:T(8,128)} %convolution_bitcast_fusion.2, f32[1,2,322,512]{3,2,1,0:T(8,128)} %convolution_bitcast_fusion.3, ...), kind=kLoop, calls=%fused_computation.27 | loop fusion | flops 8519680 | bytes 36700160 | tf_op jit(solution)/shard_map/cond/branch_1_fun/add | solution.py:54
  567.6 13.4 %fusion.115 = f32[320,512]{1,0:T(8,128)S(1)} fusion(f32[1,2,320,512]{3,2,1,0:T(8,128)} %get-tuple-element.34, f32[1,2,322,512]{3,2,1,0:T(8,128)S(1)} %convolution_bitcast_fusion.27, f32[1,2,322,512]{3,2,1,0:T(8,128)S(1)} %convolution_bitcast_fusion.28, f32[1,2,322,512]{3,2,1,0:T(8,128)} %convolution_bitcast_fusion.29, ...), kind=kLoop, calls=%fused_computation.199 | loop fusion | flops 9011200 | bytes 37355520 | tf_op jit(solution)/shard_map/reduce_sum | solution.py:60
  581.4 0.8 reduce_sum.96
  582.4 73.4 %all-reduce.1 = (f32[512]{0:T(512)S(1)}, f32[512]{0:T(512)S(1)}) all-reduce(f32[512]{0:T(512)S(1)} %get-tuple-element.18, f32[512]{0:T(512)S(1)} %get-tuple-element.17), channel_id=1, replica_groups=mesh['tm'=4,'rows'=64] {'tm','rows'}, use_global_device_ids=true, to_apply=%region_14.15 | all-reduce | flops 1024 | bytes 8192 | tf_op jit(solution)/shard_map/psum | solution.py:109
  655.7 0.6 broadcast_multiply_fusion
  657.1 0.8 fusion.131
  (48 shorter events, 7.1 us)
Async XLA Ops:
  17.8 14.3 %copy-start.1 = (bf16[1,2,320,512]{3,2,1,0:T(8,128)(2,1)S(1)}, bf16[1,2,320,512]{3,2,1,0:T(8,128)(2,1)}, u32[]{:S(2)}) copy-start(bf16[1,2,320,512]{3,2,1,0:T(8,128)(2,1)} %param.11) | copy-start | bytes 1966084
  17.8 458.0 %all-to-all-start = ((bf16[64,3,3,3,8,512]{5,4,3,2,1,0:T(8,128)(2,1)}), bf16[64,3,3,3,8,512]{5,4,3,2,1,0:T(8,128)(2,1)}, u32[]{:S(2)}, u32[]{:S(2)}) async-start(bf16[64,3,3,3,8,512]{5,4,3,2,1,0:T(8,128)(2,1)} %stack.2), calls=%async_computation | async-start | bytes 28311552 | tf_op jit(solution)/shard_map/all_to_all | solution.py:12
  32.2 312.0 %copy-start.2 = (bf16[1,1,160,512]{3,2,1,0:T(8,128)(2,1)S(1)}, bf16[1,1,160,512]{3,2,1,0:T(8,128)(2,1)}, u32[]{:S(2)}) copy-start(bf16[1,1,160,512]{3,2,1,0:T(8,128)(2,1)} %param.7) | copy-start | bytes 491524
  32.2 307.2 %collective-permute-start = (bf16[1,1,320,512]{3,2,1,0:T(8,128)(2,1)S(1)}, bf16[1,1,320,512]{3,2,1,0:T(8,128)(2,1)S(1)}, u32[]{:S(2)}, u32[]{:S(2)}) collective-permute-start(bf16[1,1,320,512]{3,2,1,0:T(8,128)(2,1)S(1)} %get-tuple-element.27), channel_id=1, source_target_pairs={{0,1},{1,2},{2,3},{3,4},{4,5},{5,6},{6,7},{7,8},{8,9},{9,10},{10,1... | collective-permute-start | bytes 983048 | tf_op jit(solution)/shard_map/ppermute | solution.py:21
  35.9 305.7 %collective-permute-start.1 = (bf16[1,1,320,512]{3,2,1,0:T(8,128)(2,1)S(1)}, bf16[1,1,320,512]{3,2,1,0:T(8,128)(2,1)S(1)}, u32[]{:S(2)}, u32[]{:S(2)}) collective-permute-start(bf16[1,1,320,512]{3,2,1,0:T(8,128)(2,1)S(1)} %get-tuple-element.26), channel_id=1, source_target_pairs={{1,0},{2,1},{3,2},{4,3},{5,4},{6,5},{7,6},{8,7},{9,8},{10,9},{11,1... | collective-permute-start | bytes 983048 | tf_op jit(solution)/shard_map/ppermute | solution.py:24
  341.6 130.5 %collective-permute-start.3 = (bf16[1,4,320,512]{3,2,1,0:T(8,128)(2,1)S(1)}, bf16[1,4,320,512]{3,2,1,0:T(8,128)(2,1)S(1)}, u32[]{:S(2)}, u32[]{:S(2)}) collective-permute-start(bf16[1,4,320,512]{3,2,1,0:T(8,128)(2,1)S(1)} %constant_dynamic-update-slice_fusion), channel_id=1, source_target_pairs={{128,0},{192,64},{129,1},{193,65},{130,2},{194,66},{131,3},{195,67... | collective-permute-start | bytes 3932168 | tf_op jit(solution)/shard_map/ppermute | solution.py:32
  342.9 129.2 %collective-permute-start.2 = (bf16[1,4,320,512]{3,2,1,0:T(8,128)(2,1)S(1)}, bf16[1,4,320,512]{3,2,1,0:T(8,128)(2,1)}, u32[]{:S(2)}, u32[]{:S(2)}) collective-permute-start(bf16[1,4,320,512]{3,2,1,0:T(8,128)(2,1)S(1)} %constant_dynamic-update-slice_fusion), channel_id=1, source_target_pairs={{64,0},{128,64},{192,128},{65,1},{129,65},{193,129},{66,2},{130,66... | collective-permute-start | bytes 3932168 | tf_op jit(solution)/shard_map/ppermute | solution.py:32
  475.8 7.0 %copy-start = (bf16[3,4,322,512]{3,2,1,0:T(8,128)(2,1)S(1)}, bf16[3,4,322,512]{3,2,1,0:T(8,128)(2,1)}, u32[]{:S(2)}) copy-start(bf16[3,4,322,512]{3,2,1,0:T(8,128)(2,1)} %fusion.113) | copy-start | bytes 11870212
  581.0 1.2 copy-start.3
  581.0 1.2 copy-start.4
